TPU v7x, 512 devices: a whole 4x4x16 slice. The times are simulated.
512 devices in a mesh: mom: 32 (over z, core), hist: 16 (over y, x).
Axes of the slice: x: 4, y: 4, z: 16, core: 2. Of those that a mesh axis runs over, the one named last changes fastest.
Arguments:
- green_hist: float32 [2, 2, 2, 4096, 4096], P(None, None, None, 'mom', 'hist'), may hold values from 0.5 to 1.5
- sigma_row: float32 [2, 2, 2, 4096], P(None, None, None, 'hist'), may hold values from -6 to 6
- coupling_row: float32 [2, 2, 2, 4096], P(None, None, None, 'hist'), may hold values from -3 to 3
- prop_prev: float32 [2, 2, 2, 4096], P(None, None, None, 'mom'), may hold values from 0.5 to 1.5
- init_state: float32 [4], replicated, may hold values from 0.5 to 1.5
- state_rates: float32 [4], replicated, may hold values from 0.05 to 2
- source_row: float32 [4, 4096], P(None, 'hist'), may hold values from -6 to 6
- mom_ids: int32 [4096], P('mom'), may hold values from 0 to 4095, each once
- t_step: int32 [1], replicated, may hold values from 0 to 2999
- block_len: int32 [16], replicated, may hold values from 1 to 256, 2560 in all
Outputs:
- prop_new: float32 [2, 2, 2, 4096], P(None, None, None, 'mom')
- pp_row: float32 [4, 4096], P(None, 'hist')
- hyb_row: float32 [2, 2, 2, 4096], P(None, None, None, 'hist')
Inputs may be any that keep to these rules, and one draw needn't show every extreme that they name: `mom_ids`: each momentum point 0 .. 4095 appears once. `block_len`: the entries sum to 2560; the largest is 256.
All inputs are finite; a program needn't handle non-finite values.
Results may differ from a plain program's by a relative error of at most 0.00035.
Values sent between devices are 32-bit elements; how exact they have to be, the bound alone decides.
A program may use at most 64 MiB of HBM per device.

v0:
```python
import math
import jax
import jax.numpy as jnp
import numpy as np
from jax import lax
from jax.sharding import PartitionSpec as P

LK = 64
TIME_STEP = 0.005
HOPPING_TIME = 0.5
FIELD_STEP = 0.0025


def entering(value, axis, join, neutral):
    count, mine = (lax.axis_size(axis), lax.axis_index(axis))
    pieces = jax.tree.map(lambda part: lax.all_gather(part, axis), value)
    so_far = jax.tree.map(
        lambda part, zero: jnp.full_like(part, 0) + jnp.asarray(zero, part.dtype), value, neutral
    )

    def step(position, so_far):
        longer = join(so_far, jax.tree.map(lambda part: part[position], pieces))
        return jax.tree.map(lambda new, old: jnp.where(position < mine, new, old), longer, so_far)

    return lax.fori_loop(0, count - 1, step, so_far)


def from_root(value, axis, source):
    kept = jnp.where(lax.axis_index(axis) == source, value, 0).astype(value.dtype)
    return lax.psum(kept, axis)


def parity_sign(value):
    sign_value = 1
    for position in range(4):
        if value >> position & 1:
            sign_value = -sign_value
    return sign_value


def fock_table():
    table = np.zeros((2, 2, 4, 4), np.float32)
    for state_in in range(4):
        for orb_b in range(2):
            if state_in >> orb_b & 1:
                sign_b = parity_sign(state_in & (1 << orb_b) - 1)
                middle = state_in ^ 1 << orb_b
                for orb_a in range(2):
                    if not middle >> orb_a & 1:
                        sign_a = parity_sign(middle & (1 << orb_a) - 1)
                        state_out = middle | 1 << orb_a
                        table[orb_a, orb_b, state_out, state_in] += sign_a * sign_b
    return jnp.asarray(table, jnp.float32)


def complex_product(left, right):
    hp = lax.Precision.HIGHEST
    real_part = jnp.einsum("ab...,bc...->ac...", left[0], right[0], precision=hp) - jnp.einsum(
        "ab...,bc...->ac...", left[1], right[1], precision=hp
    )
    imag_part = jnp.einsum("ab...,bc...->ac...", left[0], right[1], precision=hp) + jnp.einsum(
        "ab...,bc...->ac...", left[1], right[0], precision=hp
    )
    return jnp.stack([real_part, imag_part])


def memory_sum(weighted, history):
    hp = lax.Precision.HIGHEST
    real_part = jnp.einsum("abs,bcks->ack", weighted[0], history[0], precision=hp) - jnp.einsum(
        "abs,bcks->ack", weighted[1], history[1], precision=hp
    )
    imag_part = jnp.einsum("abs,bcks->ack", weighted[0], history[1], precision=hp) + jnp.einsum(
        "abs,bcks->ack", weighted[1], history[0], precision=hp
    )
    return jnp.stack([real_part, imag_part])


def row_product(current, history):
    hp = lax.Precision.HIGHEST
    real_part = jnp.einsum("ack,bcks->abs", current[0], history[0], precision=hp) + jnp.einsum(
        "ack,bcks->abs", current[1], history[1], precision=hp
    )
    imag_part = jnp.einsum("ack,bcks->abs", current[1], history[0], precision=hp) - jnp.einsum(
        "ack,bcks->abs", current[0], history[1], precision=hp
    )
    return jnp.stack([real_part, imag_part])


def momentum_phase(mom_ids, t_step, total):
    field = FIELD_STEP * t_step[0].astype(jnp.float32)
    along_x = 2.0 * math.pi * (mom_ids % LK).astype(jnp.float32) / LK
    along_y = 2.0 * math.pi * (mom_ids // LK).astype(jnp.float32) / (total // LK)
    energy = -2.0 * (jnp.cos(along_x - field) + jnp.cos(along_y - field))
    angle = HOPPING_TIME * energy
    return (jnp.cos(angle), jnp.sin(angle))


def advance(previous, memory, cosine, sine):
    summed = previous + memory
    real_part = cosine * summed[0] + sine * summed[1]
    imag_part = cosine * summed[1] - sine * summed[0]
    return jnp.stack([real_part, imag_part])


def compose(earlier, later):
    hp = lax.Precision.HIGHEST
    mats = jnp.einsum("...nm,...mk->...nk", later[0], earlier[0], precision=hp)
    vecs = jnp.einsum("...nm,...m->...n", later[0], earlier[1], precision=hp) + later[1]
    return (mats, vecs)


def on_device(
    green_hist,
    sigma_row,
    coupling_row,
    prop_prev,
    init_state,
    state_rates,
    source_row,
    mom_ids,
    t_step,
    block_len,
):
    slots_dev = green_hist.shape[-1]
    mom_dev = green_hist.shape[3]
    mom_count = lax.axis_size("mom")
    hist_count = lax.axis_size("hist")
    total = mom_dev * mom_count
    hist_pos = lax.axis_index("hist")
    length = lax.dynamic_slice_in_dim(block_len, hist_pos, 1, 0)[0]
    live_mask = jnp.arange(slots_dev, dtype=jnp.int32) < length
    weight = jnp.where(live_mask, jnp.float32(TIME_STEP), jnp.float32(0.0))
    memory_part = memory_sum(sigma_row * weight, green_hist)
    cosine, sine = momentum_phase(mom_ids, t_step, total)
    memory = lax.psum(memory_part, "hist")
    prop_new = advance(prop_prev, memory, cosine, sine)
    row_part = row_product(prop_new, green_hist) / total
    row_part = jnp.where(live_mask, row_part, jnp.float32(0.0))
    local_row = lax.psum(row_part, "mom")
    delta = complex_product(local_row, coupling_row)
    table = fock_table()
    lam = jnp.einsum("abs,abnm->snm", delta[0], table, precision=lax.Precision.HIGHEST)
    retain = jnp.diag(jnp.exp(-state_rates / (slots_dev * hist_count)))
    identity = jnp.eye(init_state.shape[0], dtype=jnp.float32)
    mats = jnp.where(live_mask[:, None, None], retain[None] - TIME_STEP * lam, identity[None])
    vecs = jnp.where(live_mask[:, None], TIME_STEP * source_row.T, jnp.float32(0.0))
    cum_mats, cum_vecs = lax.associative_scan(compose, (mats, vecs), axis=0)
    block_map = (cum_mats[-1], cum_vecs[-1])
    prior = entering(block_map, "hist", compose, (identity, jnp.zeros_like(init_state)))
    start_state = jnp.dot(prior[0], init_state, precision=lax.Precision.HIGHEST) + prior[1]
    states = (
        jnp.einsum("snm,m->sn", cum_mats, start_state, precision=lax.Precision.HIGHEST) + cum_vecs
    )
    final_state = from_root(states[-1], "hist", hist_count - 1)
    pp_row = states.T
    scale = 1.0 / jnp.sqrt(1.0 + jnp.sum(final_state * final_state))
    hyb_row = delta * scale
    return (prop_new, pp_row, hyb_row)


def solution(mesh):
    placed = (
        P(None, None, None, "mom", "hist"),
        P(None, None, None, "hist"),
        P(None, None, None, "hist"),
        P(None, None, None, "mom"),
        P(),
        P(),
        P(None, "hist"),
        P("mom"),
        P(),
        P(),
    )
    return jax.shard_map(
        on_device,
        mesh=mesh,
        in_specs=placed,
        out_specs=(P(None, None, None, "mom"), P(None, "hist"), P(None, None, None, "hist")),
        check_vma=False,
    )
```

profile of v0, /device:TPU:2, one launch (start us, length us, event | category | flops | bytes accessed | tf_op | source)
XLA Modules:
  0.0 226.2 jit_solution(4658161577168113196)
XLA Ops:
  1.3 0.6 copy-done.15
  2.0 0.6 dynamic_slice.17
  2.5 0.6 iota_compare_fusion.1
  3.2 0.7 broadcast_select_fusion.2
  3.9 0.6 copy-done.14
  4.8 0.6 copy-done.13
  6.1 0.7 copy-done.11
  7.1 1.3 fusion.111
  8.4 0.5 convolution_bitcast_fusion.8
  8.9 0.5 fusion.22
  9.5 0.5 convolution_bitcast_fusion.6
  10.0 0.5 fusion.21
  10.6 41.4 %psum.21 = f32[2,2,2,128]{3,1,2,0:T(2,128)S(1)} all-reduce(f32[2,2,2,128]{3,1,2,0:T(2,128)S(1)} %pad_maximum_fusion.6), channel_id=1, replica_groups=mesh['mom'=32,'hist'=16] {'hist'}, use_global_device_ids=true, to_apply=%region_0.1 | all-reduce | flops 1024 | bytes 8192 | tf_op jit(solution)/shard_map/psum | solution.py:135
  52.3 0.4 fusion.18
  52.7 0.6 copy.173
  53.6 0.4 fusion.16
  54.0 48.5 %psum.22 = f32[2,2,2,256]{3,1,2,0:T(2,128)S(1)} all-reduce(f32[2,2,2,256]{3,1,2,0:T(2,128)S(1)} %fusion.70), channel_id=1, replica_groups=mesh['mom'=32,'hist'=16] {'mom'}, use_global_device_ids=true, to_apply=%region_1.2 | all-reduce | flops 2048 | bytes 16384 | tf_op jit(solution)/shard_map/psum | solution.py:139
  102.9 1.8 fusion.28
  104.7 1.8 fusion.32
  106.5 1.9 convolution_subtract_fusion
  108.4 1.9 fusion.11
  110.6 0.6 copy-done.17
  112.6 0.4 slice.296
  113.6 1.0 fusion.113
  115.3 0.6 fusion.38
  116.5 0.4 fusion.46
  120.8 0.7 slice-done.5
  122.3 0.7 slice-done.4
  123.9 0.6 slice-done.3
  125.6 0.6 slice-done.2
  127.7 0.6 slice-done.1
  129.0 0.7 slice-done.6
  130.4 21.8 %all-gather = f32[16,1,4]{2,1,0:T(1,128)S(1)} all-gather(f32[1,1,4]{2,1,0:T(1,128)S(1)} %bitcast.255), channel_id=1, replica_groups=mesh['mom'=32,'hist'=16] {'hist'}, dimensions={0}, use_global_device_ids=true | all-gather | bytes 272 | tf_op jit(solution)/shard_map/all_gather | solution.py:16
  152.1 0.4 pad.108
  152.5 0.4 pad.109
  152.9 0.6 fusion.40
  153.6 0.6 slice-done
  154.2 0.8 pad.110
  155.1 0.8 pad.111
  156.1 1.0 fusion.34
  157.2 1.7 pad.112
  158.9 1.7 pad.113
  160.5 21.1 %all_gather.6 = f32[16,4,4]{2,1,0:T(4,128)S(1)} all-gather(f32[1,4,4]{2,1,0:T(4,128)S(1)} %slice_add_fusion), channel_id=1, replica_groups=mesh['mom'=32,'hist'=16] {'hist'}, dimensions={0}, use_global_device_ids=true | all-gather | bytes 1088 | tf_op jit(solution)/shard_map/all_gather | solution.py:16
  181.7 4.4 %while.16 = (s32[]{:T(128)}, f32[4,4]{1,0:T(4,128)S(1)}, f32[4]{0:T(128)S(1)}, s32[]{:T(128)}, f32[16,4,4]{2,1,0:T(4,128)S(1)}, /*index=5*/f32[16,4]{1,0:T(8,128)S(1)}, s32[]{:T(128)}, s32[]{:T(128)}) while((s32[]{:T(128)}, f32[4,4]{1,0:T(4,128)S(1)}, f32[4]{0:T(128)S(1)}, s32[]{:T(128)}, f32[16,4,4]{2,1,0:T(4,128)S(1)}, ...), condition=%wide.region_3.4_spmd.clone, body=%wide.region_2.3_spmd.clone.sunk | while | flops 996 | bytes 12644 | solution.py:25
  186.2 0.4 multiply_reduce_fusion
  186.9 37.5 %psum.23 = f32[4]{0:T(128)S(1)} all-reduce(f32[4]{0:T(128)S(1)} %fusion.86), channel_id=1, replica_groups=mesh['mom'=32,'hist'=16] {'hist'}, use_global_device_ids=true, to_apply=%region_4.5 | all-reduce | flops 4 | bytes 32 | tf_op jit(solution)/shard_map/psum | solution.py:30
  224.3 0.6 multiply_reduce_fusion.14
  225.6 0.6 maximum_multiply_fusion.1
  (269 shorter events, 20.6 us)
Async XLA Ops:
  0.6 185.4 %copy-start = (f32[4]{0:T(128)S(1)}, f32[4]{0:T(128)}, u32[]{:S(2)}) copy-start(f32[4]{0:T(128)} %param.17) | copy-start | bytes 52
  1.3 0.7 copy-start.15
  3.2 0.7 copy-start.16
  3.9 0.7 copy-start.14
  4.7 0.7 copy-start.13
  5.4 0.7 copy-start.8
  5.4 0.7 copy-start.10
  6.1 0.7 copy-start.11
  8.4 43.5 %copy-start.1 = (f32[2,2,2,128,256]{4,3,2,1,0:T(8,128)S(1)}, f32[2,2,2,128,256]{4,3,2,1,0:T(8,128)}, u32[]{:S(2)}) copy-start(f32[2,2,2,128,256]{4,3,2,1,0:T(8,128)} %param.13) | copy-start | bytes 3145732
  10.5 41.4 %copy-start.12 = (f32[2,2,2,128]{3,2,1,0:T(2,128)S(1)}, f32[2,2,2,128]{3,2,1,0:T(2,128)}, u32[]{:S(2)}) copy-start(f32[2,2,2,128]{3,2,1,0:T(2,128)} %param.16) | copy-start | bytes 12292
  110.5 0.7 copy-start.17
  114.5 38.4 %copy-start.2 = (f32[128,4,4]{2,1,0:T(4,128)}, f32[128,4,4]{2,1,0:T(4,128)S(1)}, u32[]{:S(2)}) copy-start(f32[128,4,4]{2,1,0:T(4,128)S(1)} %fusion.113) | copy-start | bytes 24580
  115.8 11.5 %copy-start.3 = (f32[64,4,4]{2,1,0:T(4,128)}, f32[64,4,4]{2,1,0:T(4,128)S(1)}, u32[]{:S(2)}) copy-start(f32[64,4,4]{2,1,0:T(4,128)S(1)} %fusion.38) | copy-start | bytes 12292
  116.8 8.5 %copy-start.4 = (f32[32,4,4]{2,1,0:T(4,128)}, f32[32,4,4]{2,1,0:T(4,128)S(1)}, u32[]{:S(2)}) copy-start(f32[32,4,4]{2,1,0:T(4,128)S(1)} %fusion.46) | copy-start | bytes 6148
  117.7 6.0 %copy-start.5 = (f32[16,4,4]{2,1,0:T(4,128)}, f32[16,4,4]{2,1,0:T(4,128)S(1)}, u32[]{:S(2)}) copy-start(f32[16,4,4]{2,1,0:T(4,128)S(1)} %fusion.54) | copy-start | bytes 3076
  118.4 3.7 %copy-start.6 = (f32[8,4,4]{2,1,0:T(4,128)}, f32[8,4,4]{2,1,0:T(4,128)S(1)}, u32[]{:S(2)}) copy-start(f32[8,4,4]{2,1,0:T(4,128)S(1)} %fusion.62) | copy-start | bytes 1540
  119.1 1.5 copy-start.7
  120.7 0.7 slice-start.5
  122.3 0.7 slice-start.4
  123.8 0.7 slice-start.3
  125.6 0.7 slice-start.2
  127.7 0.7 slice-start.1
  129.0 0.7 slice-start.6
  153.5 0.7 slice-start
  186.7 38.9 %copy-start.9 = (f32[256,4]{0,1:T(4,128)}, f32[256,4]{0,1:T(4,128)S(1)}, u32[]{:S(2)}) copy-start(f32[256,4]{0,1:T(4,128)S(1)} %add_add_fusion) | copy-start | bytes 12292
where the time goes:
time: 227 us; the launch traced here: 226 us
  blocking collectives  170 us (75%)
  local copies, waits for them, and re-layouts  26.3 us (12%)
  matrix products  21.2 us (9%)
  other arithmetic  5.78 us (3%)
  between operations  2.72 us (1%)
    psum x1, blocking collectives, on_device(): local_row = lax.psum(row_part, 'mom')  48.5 us
    all_gather x2, blocking collectives, entering(): pieces = jax.tree.map(lambda part: lax.all_gather(part, axis), value)  42.9 us
    psum x1, blocking collectives, on_device(): memory = lax.psum(memory_part, 'hist')  41.4 us
    psum x1, blocking collectives, from_root(): return lax.psum(kept, axis)  37.5 us
    slice x45, local copies, waits for them, and re-layouts, on_device(): cum_mats, cum_vecs = lax.associative_scan(compose, (mats, vecs), axis=0)  9.1 us
    pad x28, local copies, waits for them, and re-layouts, on_device(): cum_mats, cum_vecs = lax.associative_scan(compose, (mats, vecs), axis=0)  8.22 us
    dot_general x30, matrix products, compose(): mats = jnp.einsum('...nm,...mk->...nk', later[0], earlier[0], precision=hp)  7.39 us
    unnamed x50, local copies, waits for them, and re-layouts  5.18 us

commit v1 on v0

--- a/solution.py
+++ b/solution.py
@@ -136,7 +136,7 @@
     prop_new = advance(prop_prev, memory, cosine, sine)
     row_part = row_product(prop_new, green_hist) / total
     row_part = jnp.where(live_mask, row_part, jnp.float32(0.0))
-    local_row = lax.psum(row_part, "mom")
+    local_row = jnp.sum(lax.all_gather(row_part, "mom"), axis=0)
     delta = complex_product(local_row, coupling_row)
     table = fock_table()
     lam = jnp.einsum("abs,abnm->snm", delta[0], table, precision=lax.Precision.HIGHEST)

time: 227 us -> 211 us (0.930)
  the two profiles are of different devices: /device:TPU:2 before, /device:TPU:32 now
where the time goes in v1:
time: 211 us; the launch traced here: 210 us
  blocking collectives  154 us (73%)
  local copies, waits for them, and re-layouts  26.4 us (13%)
  matrix products  20.9 us (10%)
  other arithmetic  5.94 us (3%)
  between operations  2.72 us (1%)
    psum x1, blocking collectives, on_device(): memory = lax.psum(memory_part, 'hist')  40.7 us
    all_gather x2, blocking collectives, entering(): pieces = jax.tree.map(lambda part: lax.all_gather(part, axis), value)  40.4 us
    psum x1, blocking collectives, from_root(): return lax.psum(kept, axis)  38.1 us
    all_gather x1, blocking collectives, on_device(): local_row = jnp.sum(lax.all_gather(row_part, 'mom'), axis=0)  35 us
    slice x45, local copies, waits for them, and re-layouts, on_device(): cum_mats, cum_vecs = lax.associative_scan(compose, (mats, vecs), axis=0)  9.24 us
    pad x28, local copies, waits for them, and re-layouts, on_device(): cum_mats, cum_vecs = lax.associative_scan(compose, (mats, vecs), axis=0)  8.22 us
    dot_general x30, matrix products, compose(): mats = jnp.einsum('...nm,...mk->...nk', later[0], earlier[0], precision=hp)  7.39 us
    unnamed x52, local copies, waits for them, and re-layouts  5.54 us

profile of v1, /device:TPU:32, one launch (start us, length us, event | category | flops | bytes accessed | tf_op | source)
XLA Modules:
  0.0 210.3 jit_solution(7038498421506635376)
XLA Ops:
  1.3 0.6 copy-done.15
  2.0 0.6 dynamic_slice.17
  2.5 0.6 iota_compare_fusion.1
  3.2 0.7 broadcast_select_fusion.2
  3.9 0.6 copy-done.14
  4.8 0.6 copy-done.13
  6.1 0.7 copy-done.11
  7.1 1.3 fusion.115
  8.4 0.5 convolution_bitcast_fusion.8
  8.9 0.5 fusion.22
  9.5 0.5 convolution_bitcast_fusion.6
  10.0 0.5 fusion.21
  10.6 40.7 %psum.14 = f32[2,2,2,128]{3,1,2,0:T(2,128)S(1)} all-reduce(f32[2,2,2,128]{3,1,2,0:T(2,128)S(1)} %pad_maximum_fusion.6), channel_id=1, replica_groups=mesh['mom'=32,'hist'=16] {'hist'}, use_global_device_ids=true, to_apply=%region_0.1 | all-reduce | flops 1024 | bytes 8192 | tf_op jit(solution)/shard_map/psum | solution.py:135
  51.6 0.4 fusion.18
  52.0 0.6 copy.169
  53.0 0.4 fusion.16
  53.4 35.0 %all_gather.10 = f32[32,2,2,2,256]{4,3,2,1,0:T(2,128)S(1)} all-gather(f32[1,2,2,2,256]{4,3,2,1,0:T(2,128)S(1)} %copy.152), channel_id=1, replica_groups=mesh['mom'=32,'hist'=16] {'mom'}, dimensions={0}, use_global_device_ids=true | all-gather | bytes 270336 | tf_op jit(solution)/shard_map/all_gather | solution.py:139
  88.8 1.8 fusion.28
  90.7 1.8 fusion.34
  92.5 1.9 convolution_subtract_fusion
  94.3 1.9 fusion.11
  96.6 0.6 copy-done.17
  98.6 0.4 slice.296
  99.5 1.0 fusion.118
  101.2 0.6 fusion.42
  102.4 0.4 fusion.50
  106.7 0.7 slice-done.5
  108.2 0.7 slice-done.4
  109.8 0.6 slice-done.3
  111.5 0.6 slice-done.2
  113.6 0.6 slice-done.1
  114.9 0.7 slice-done.6
  116.3 17.0 %all-gather = f32[16,1,4]{2,1,0:T(1,128)S(1)} all-gather(f32[1,1,4]{2,1,0:T(1,128)S(1)} %bitcast.257), channel_id=1, replica_groups=mesh['mom'=32,'hist'=16] {'hist'}, dimensions={0}, use_global_device_ids=true | all-gather | bytes 272 | tf_op jit(solution)/shard_map/all_gather | solution.py:16
  133.2 0.4 pad.108
  133.7 0.4 pad.109
  134.1 0.6 fusion.44
  134.7 0.6 slice-done
  135.4 0.8 pad.110
  136.2 0.8 pad.111
  137.2 1.0 fusion.38
  138.4 1.7 pad.112
  140.0 1.7 pad.113
  141.7 23.4 %all_gather.11 = f32[16,4,4]{2,1,0:T(4,128)S(1)} all-gather(f32[1,4,4]{2,1,0:T(4,128)S(1)} %slice_add_fusion), channel_id=1, replica_groups=mesh['mom'=32,'hist'=16] {'hist'}, dimensions={0}, use_global_device_ids=true | all-gather | bytes 1088 | tf_op jit(solution)/shard_map/all_gather | solution.py:16
  165.1 4.4 %while.16 = (s32[]{:T(128)}, f32[4,4]{1,0:T(4,128)S(1)}, f32[4]{0:T(128)S(1)}, s32[]{:T(128)}, f32[16,4,4]{2,1,0:T(4,128)S(1)}, /*index=5*/f32[16,4]{1,0:T(8,128)S(1)}, s32[]{:T(128)}, s32[]{:T(128)}) while((s32[]{:T(128)}, f32[4,4]{1,0:T(4,128)S(1)}, f32[4]{0:T(128)S(1)}, s32[]{:T(128)}, f32[16,4,4]{2,1,0:T(4,128)S(1)}, ...), condition=%wide.region_3.4_spmd.clone, body=%wide.region_2.3_spmd.clone.sunk | while | flops 996 | bytes 12644 | solution.py:25
  169.6 0.4 multiply_reduce_fusion
  170.3 38.1 %psum.15 = f32[4]{0:T(128)S(1)} all-reduce(f32[4]{0:T(128)S(1)} %fusion.90), channel_id=1, replica_groups=mesh['mom'=32,'hist'=16] {'hist'}, use_global_device_ids=true, to_apply=%region_4.5 | all-reduce | flops 4 | bytes 32 | tf_op jit(solution)/shard_map/psum | solution.py:30
  208.4 0.6 multiply_reduce_fusion.14
  209.7 0.6 maximum_multiply_fusion.1
  (271 shorter events, 20.6 us)
Async XLA Ops:
  0.6 168.8 %copy-start = (f32[4]{0:T(128)S(1)}, f32[4]{0:T(128)}, u32[]{:S(2)}) copy-start(f32[4]{0:T(128)} %param.17) | copy-start | bytes 52
  1.3 0.7 copy-start.15
  3.2 0.7 copy-start.16
  3.9 0.7 copy-start.14
  4.7 0.7 copy-start.13
  5.4 0.7 copy-start.8
  5.4 0.7 copy-start.10
  6.1 0.7 copy-start.11
  8.4 42.8 %copy-start.1 = (f32[2,2,2,128,256]{4,3,2,1,0:T(8,128)S(1)}, f32[2,2,2,128,256]{4,3,2,1,0:T(8,128)}, u32[]{:S(2)}) copy-start(f32[2,2,2,128,256]{4,3,2,1,0:T(8,128)} %param.13) | copy-start | bytes 3145732
  10.5 40.7 %copy-start.12 = (f32[2,2,2,128]{3,2,1,0:T(2,128)S(1)}, f32[2,2,2,128]{3,2,1,0:T(2,128)}, u32[]{:S(2)}) copy-start(f32[2,2,2,128]{3,2,1,0:T(2,128)} %param.16) | copy-start | bytes 12292
  96.4 0.7 copy-start.17
  100.5 33.6 %copy-start.2 = (f32[128,4,4]{2,1,0:T(4,128)}, f32[128,4,4]{2,1,0:T(4,128)S(1)}, u32[]{:S(2)}) copy-start(f32[128,4,4]{2,1,0:T(4,128)S(1)} %fusion.118) | copy-start | bytes 24580
  101.8 11.4 %copy-start.3 = (f32[64,4,4]{2,1,0:T(4,128)}, f32[64,4,4]{2,1,0:T(4,128)S(1)}, u32[]{:S(2)}) copy-start(f32[64,4,4]{2,1,0:T(4,128)S(1)} %fusion.42) | copy-start | bytes 12292
  102.8 8.4 %copy-start.4 = (f32[32,4,4]{2,1,0:T(4,128)}, f32[32,4,4]{2,1,0:T(4,128)S(1)}, u32[]{:S(2)}) copy-start(f32[32,4,4]{2,1,0:T(4,128)S(1)} %fusion.50) | copy-start | bytes 6148
  103.6 5.9 %copy-start.5 = (f32[16,4,4]{2,1,0:T(4,128)}, f32[16,4,4]{2,1,0:T(4,128)S(1)}, u32[]{:S(2)}) copy-start(f32[16,4,4]{2,1,0:T(4,128)S(1)} %fusion.58) | copy-start | bytes 3076
  104.5 3.5 %copy-start.6 = (f32[8,4,4]{2,1,0:T(4,128)}, f32[8,4,4]{2,1,0:T(4,128)S(1)}, u32[]{:S(2)}) copy-start(f32[8,4,4]{2,1,0:T(4,128)S(1)} %fusion.66) | copy-start | bytes 1540
  105.2 1.3 copy-start.7
  106.6 0.7 slice-start.5
  108.2 0.7 slice-start.4
  109.7 0.7 slice-start.3
  111.5 0.7 slice-start.2
  113.6 0.7 slice-start.1
  114.9 0.7 slice-start.6
  134.6 0.7 slice-start
  170.1 39.6 %copy-start.9 = (f32[256,4]{0,1:T(4,128)}, f32[256,4]{0,1:T(4,128)S(1)}, u32[]{:S(2)}) copy-start(f32[256,4]{0,1:T(4,128)S(1)} %add_add_fusion) | copy-start | bytes 12292
